TPU v7x, 256 devices: a whole 4x4x8 slice. The times are simulated.
256 devices in a mesh: lx: 8 (over z), ly: 8 (over x, y_lo), blk: 4 (over y_hi, core).
Axes of the slice: x: 4, y: 4 (y_hi: 2, y_lo: 2; y = y_hi * 2 + y_lo), z: 8, core: 2. Of those that a mesh axis runs over, the one named last changes fastest.
Arguments:
- block_vectors: float32 [32, 1024, 2048], P('blk', 'lx', 'ly'), may hold values from -6 to 6
- search_vectors: float32 [256, 1024, 2048], P('blk', 'lx', 'ly'), may hold values from -6 to 6
- onsite_energy: float32 [1024, 2048], P('lx', 'ly'), may hold values from -1 to 1
- site_mask: int32 [1024, 2048], P('lx', 'ly'), may hold values 0 or 1
- filter_coefs: float32 [5], replicated, may hold values from -1 to 1
Outputs:
- projected: float32 [2, 32, 256], P(None, None, 'blk')
Inputs may be any that keep to these rules, and one draw needn't show every extreme that they name: `site_mask`: 1 marks a present site, 0 a vacancy.
All inputs are finite; a program needn't handle non-finite values. No bound on the sum of `site_mask` on one device may be relied on, other than what follows from the above.
Results may differ from a plain program's by a relative error of at most 0.00016.
Values sent between devices are 32-bit elements; how exact they have to be, the bound alone decides.
No kernel may reach another device: no remote copies, remote signals or barrier semaphores. Data moves between devices by JAX's collectives and lax.ppermute only.
A program may use at most 64 MiB of HBM per device.

v0:
```python
import math
import jax
import jax.numpy as jnp
from jax import lax
from jax.sharding import PartitionSpec as P


def extended(block, sides, width):
    for axis, dim in sides:
        count = lax.axis_size(axis)
        forward = [(i, i + 1) for i in range(count - 1)]
        backward = [(target, source) for source, target in forward]
        low = lax.ppermute(
            lax.slice_in_dim(block, block.shape[dim] - width, None, axis=dim), axis, forward
        )
        high = lax.ppermute(lax.slice_in_dim(block, 0, width, axis=dim), axis, backward)
        block = jnp.concatenate([low, block, high], axis=dim)
    return block


def scaled_step(padded, onsite, present):
    nrows, ncols = onsite.shape
    row_index = lax.broadcasted_iota(jnp.int32, (nrows, ncols), 0)
    col_index = lax.broadcasted_iota(jnp.int32, (nrows, ncols), 1)
    even_sites = (row_index + col_index) % 2 == 0
    centre = padded[..., 1:-1, 1:-1]
    left_side = padded[..., 1:-1, :-2]
    right_side = padded[..., 1:-1, 2:]
    upper_side = padded[..., :-2, 1:-1]
    lower_side = padded[..., 2:, 1:-1]
    vertical = jnp.where(even_sites, lower_side, upper_side)
    return present * (onsite * centre - (left_side + right_side + vertical)) * 0.25


def gram_rows(stacked, search_vectors):
    stacks, members, nrows, ncols = stacked.shape
    flat = stacked.reshape(stacks * members, nrows * ncols)
    search_flat = search_vectors.reshape(search_vectors.shape[0], nrows * ncols)
    result = lax.dot_general(
        flat,
        search_flat,
        (((1,), (1,)), ((), ())),
        precision=lax.Precision.HIGHEST,
        preferred_element_type=jnp.float32,
    )
    return result.reshape(stacks, members, search_vectors.shape[0])


def shards(block_vectors, search_vectors, onsite_energy, site_mask, filter_coefs):
    present = site_mask.astype(jnp.float32)
    current = block_vectors * present
    filtered = filter_coefs[0] * current
    degree = filter_coefs.shape[0] - 1
    before = current
    for order in range(1, degree + 1):
        padded_field = extended(current, (("lx", 1), ("ly", 2)), 1)
        image = scaled_step(padded_field, onsite_energy, present)
        following = image if order == 1 else 2.0 * image - before
        before, current = (current, following)
        filtered = filtered + filter_coefs[order] * current
    nrows, ncols = onsite_energy.shape
    scale_factor = 1.0 / math.sqrt(nrows * ncols * lax.axis_size("lx") * lax.axis_size("ly"))
    padded_field = extended(filtered, (("lx", 1), ("ly", 2)), 1)
    image = scaled_step(padded_field, onsite_energy, present)
    paired = jnp.stack([filtered, image])
    partial_gram = gram_rows(lax.all_gather(paired, "blk", axis=1, tiled=True), search_vectors)
    total = lax.psum(partial_gram, ("lx", "ly"))
    return total * scale_factor


def solution(mesh):
    placed = (P("blk", "lx", "ly"), P("blk", "lx", "ly"), P("lx", "ly"), P("lx", "ly"), P())
    return jax.shard_map(
        shards, mesh=mesh, in_specs=placed, out_specs=P(None, None, "blk"), check_vma=False
    )
```

profile of v0, /device:TPU:16, one launch (start us, length us, event | category | flops | bytes accessed | tf_op | source)
XLA Modules:
  0.0 537.4 jit_solution(5126460402475514423)
XLA Ops:
  7.5 1.8 copy_multiply_fusion
  10.6 4.5 collective-permute-start
  15.2 1.3 collective-permute-done
  18.8 4.5 collective-permute-start.2
  23.4 1.3 collective-permute-done.2
  27.1 1.9 broadcast_multiply_fusion
  30.3 4.8 collective-permute-start.4
  35.2 1.3 collective-permute-done.4
  37.6 1.4 copy.13
  40.6 4.8 collective-permute-start.6
  49.2 2.6 fusion.34
  53.1 4.8 collective-permute-start.8
  58.0 1.3 collective-permute-done.8
  60.4 1.4 copy.17
  61.8 5.0 collective-permute-start.10
  68.8 5.0 collective-permute-done.11
  75.0 1.8 fusion.27
  78.1 4.9 collective-permute-start.12
  83.1 1.3 collective-permute-done.12
  85.5 1.4 copy.21
  88.5 5.4 %collective-permute-start.14 = (f32[8,130,1]{1,0,2:T(8,128)S(1)}, f32[8,130,1]{1,0,2:T(8,128)S(1)}, u32[]{:S(2)}, u32[]{:S(2)}) collective-permute-start(f32[8,130,1]{1,0,2:T(8,128)S(1)} %copy.21), channel_id=1, source_target_pairs={{0,4},{4,8},{8,12},{12,16},{16,20},{20,24},{24,28},{1,5},{5,9},{9,... | collective-permute-start | bytes 12488 | tf_op jit(solution)/shard_map/ppermute | solution.py:13
  97.7 8.3 %fusion.20 = f32[8,128,256]{2,0,1:T(8,128)S(1)} fusion(f32[8,128,256]{2,0,1:T(8,128)S(1)} %fusion.34, f32[8,128,256]{2,0,1:T(8,128)} %copy-done, f32[8,1,256]{2,0,1:T(8,128)S(1)} %collective-permute-done.12, f32[8,1,256]{2,0,1:T(8,128)S(1)} %collective-permute-done.13, f32[8,130,1]{2,0,1:T(8,128)} %copy.24, f32[8,130,1]{2,0,1:T(8,128)} %copy.22, ...), kind=kLoop, calls=%fused_computation.33 | loop fusion | flops 6815744 | bytes 5562516 | tf_op jit(solution)/shard_map/add | solution.py:60
  107.3 6.0 %collective-permute-start.16 = (f32[8,1,256]{2,0,1:T(8,128)S(1)}, f32[8,1,256]{2,0,1:T(8,128)S(1)}, u32[]{:S(2)}, u32[]{:S(2)}) collective-permute-start(f32[8,1,256]{2,0,1:T(8,128)S(1)} %get-tuple-element.18), channel_id=1, source_target_pairs={{0,32},{32,64},{64,96},{96,128},{128,160},{160,192},{192,224},{1,3... | collective-permute-start | bytes 24584 | tf_op jit(solution)/shard_map/ppermute | solution.py:13
  113.3 1.3 collective-permute-done.16
  115.3 4.8 collective-permute-start.18
  120.5 1.5 collective-permute-start.19
  122.4 4.8 collective-permute-done.19
  128.4 1.8 fusion.11
  130.2 1.5 pad_maximum_fusion
  131.7 71.7 %all-gather.2.cloned.1.call-done = f32[2,32,128,256]{3,1,2,0:T(8,128)} async-done(((f32[2,8,128,256]{3,1,2,0:T(8,128)}), f32[2,32,128,256]{3,1,2,0:T(8,128)}) %all-gather.2.cloned.1.call-update) | async-done | bytes 8388624 | tf_op jit(solution)/shard_map/all_gather | solution.py:66
  203.4 16.7 %fusion.3 = f32[2,32,64]{2,1,0:T(8,128)S(1)} fusion(f32[2,32,128,256]{3,1,2,0:T(8,128)} %all-gather.2.cloned.1.call-done, f32[64,128,256]{2,1,0:T(8,128)} %param.6), kind=kOutput, calls=%fused_computation.4 | convolution fusion | flops 1610612736 | bytes 16793600 | tf_op jit(solution)/shard_map/dot_general | solution.py:39
  220.0 309.9 %psum.7 = f32[2,32,64]{2,1,0:T(8,128)S(1)} all-reduce(f32[2,32,64]{2,1,0:T(8,128)S(1)} %fusion.3), channel_id=1, replica_groups=mesh['lx'=8,'ly'=8,'blk'=4] {'lx','ly'}, use_global_device_ids=true, to_apply=%region_0.1 | all-reduce | flops 4096 | bytes 32768 | tf_op jit(solution)/shard_map/psum | solution.py:67
  (66 shorter events, 31.8 us)
Async XLA Ops:
  6.5 196.8 %all-gather.2.cloned.1.call-start = ((), (), s32[]{:S(2)}) async-start(), calls=%async_computation | async-start | bytes 10485760 | tf_op jit(solution)/shard_map/all_gather | solution.py:66
  9.3 5.9 %collective-permute-start.1 = (f32[8,1,256]{2,0,1:T(8,128)S(1)}, f32[8,1,256]{2,0,1:T(8,128)S(1)}, u32[]{:S(2)}, u32[]{:S(2)}) collective-permute-start(f32[8,1,256]{2,0,1:T(8,128)S(1)} %get-tuple-element.25), channel_id=1, source_target_pairs={{32,0},{64,32},{96,64},{128,96},{160,128},{192,160},{224,192},{33,... | collective-permute-start | bytes 24584 | tf_op jit(solution)/shard_map/ppermute | solution.py:16
  10.6 5.9 %collective-permute-start = (f32[8,1,256]{2,0,1:T(8,128)S(1)}, f32[8,1,256]{2,0,1:T(8,128)S(1)}, u32[]{:S(2)}, u32[]{:S(2)}) collective-permute-start(f32[8,1,256]{2,0,1:T(8,128)S(1)} %get-tuple-element.26), channel_id=1, source_target_pairs={{0,32},{32,64},{64,96},{96,128},{128,160},{160,192},{192,224},{1,3... | collective-permute-start | bytes 24584 | tf_op jit(solution)/shard_map/ppermute | solution.py:13
  16.8 10.3 %copy-start.1 = (f32[128,256]{1,0:T(8,128)S(1)}, f32[128,256]{1,0:T(8,128)}, u32[]{:S(2)}) copy-start(f32[128,256]{1,0:T(8,128)} %param.7) | copy-start | bytes 393220
  17.5 8.4 %collective-permute-start.3 = (f32[8,130,1]{1,0,2:T(8,128)S(1)}, f32[8,130,1]{1,0,2:T(8,128)S(1)}, u32[]{:S(2)}, u32[]{:S(2)}) collective-permute-start(f32[8,130,1]{1,0,2:T(8,128)S(1)} %copy.11), channel_id=1, source_target_pairs={{4,0},{8,4},{12,8},{16,12},{20,16},{24,20},{28,24},{5,1},{9,5},{13... | collective-permute-start | bytes 12488 | tf_op jit(solution)/shard_map/ppermute | solution.py:16
  18.8 5.9 %collective-permute-start.2 = (f32[8,130,1]{1,0,2:T(8,128)S(1)}, f32[8,130,1]{1,0,2:T(8,128)S(1)}, u32[]{:S(2)}, u32[]{:S(2)}) collective-permute-start(f32[8,130,1]{1,0,2:T(8,128)S(1)} %copy.9), channel_id=1, source_target_pairs={{0,4},{4,8},{8,12},{12,16},{16,20},{20,24},{24,28},{1,5},{5,9},{9,... | collective-permute-start | bytes 12488 | tf_op jit(solution)/shard_map/ppermute | solution.py:13
  29.0 6.1 %collective-permute-start.5 = (f32[8,1,256]{2,0,1:T(8,128)S(1)}, f32[8,1,256]{2,0,1:T(8,128)S(1)}, u32[]{:S(2)}, u32[]{:S(2)}) collective-permute-start(f32[8,1,256]{2,0,1:T(8,128)S(1)} %get-tuple-element.23), channel_id=1, source_target_pairs={{32,0},{64,32},{96,64},{128,96},{160,128},{192,160},{224,192},{33,... | collective-permute-start | bytes 24584 | tf_op jit(solution)/shard_map/ppermute | solution.py:16
  30.3 6.2 %collective-permute-start.4 = (f32[8,1,256]{2,0,1:T(8,128)S(1)}, f32[8,1,256]{2,0,1:T(8,128)S(1)}, u32[]{:S(2)}, u32[]{:S(2)}) collective-permute-start(f32[8,1,256]{2,0,1:T(8,128)S(1)} %get-tuple-element.24), channel_id=1, source_target_pairs={{0,32},{32,64},{64,96},{96,128},{128,160},{160,192},{192,224},{1,3... | collective-permute-start | bytes 24584 | tf_op jit(solution)/shard_map/ppermute | solution.py:13
  39.3 8.7 %collective-permute-start.7 = (f32[8,130,1]{1,0,2:T(8,128)S(1)}, f32[8,130,1]{1,0,2:T(8,128)S(1)}, u32[]{:S(2)}, u32[]{:S(2)}) collective-permute-start(f32[8,130,1]{1,0,2:T(8,128)S(1)} %copy.15), channel_id=1, source_target_pairs={{4,0},{8,4},{12,8},{16,12},{20,16},{24,20},{28,24},{5,1},{9,5},{13... | collective-permute-start | bytes 12488 | tf_op jit(solution)/shard_map/ppermute | solution.py:16
  40.6 6.2 %collective-permute-start.6 = (f32[8,130,1]{1,0,2:T(8,128)S(1)}, f32[8,130,1]{1,0,2:T(8,128)S(1)}, u32[]{:S(2)}, u32[]{:S(2)}) collective-permute-start(f32[8,130,1]{1,0,2:T(8,128)S(1)} %copy.13), channel_id=1, source_target_pairs={{0,4},{4,8},{8,12},{12,16},{16,20},{20,24},{24,28},{1,5},{5,9},{9,... | collective-permute-start | bytes 12488 | tf_op jit(solution)/shard_map/ppermute | solution.py:13
  51.8 6.1 %collective-permute-start.9 = (f32[8,1,256]{2,0,1:T(8,128)S(1)}, f32[8,1,256]{2,0,1:T(8,128)S(1)}, u32[]{:S(2)}, u32[]{:S(2)}) collective-permute-start(f32[8,1,256]{2,0,1:T(8,128)S(1)} %get-tuple-element.21), channel_id=1, source_target_pairs={{32,0},{64,32},{96,64},{128,96},{160,128},{192,160},{224,192},{33,... | collective-permute-start | bytes 24584 | tf_op jit(solution)/shard_map/ppermute | solution.py:16
  53.1 6.2 %collective-permute-start.8 = (f32[8,1,256]{2,0,1:T(8,128)S(1)}, f32[8,1,256]{2,0,1:T(8,128)S(1)}, u32[]{:S(2)}, u32[]{:S(2)}) collective-permute-start(f32[8,1,256]{2,0,1:T(8,128)S(1)} %get-tuple-element.22), channel_id=1, source_target_pairs={{0,32},{32,64},{64,96},{96,128},{128,160},{160,192},{192,224},{1,3... | collective-permute-start | bytes 24584 | tf_op jit(solution)/shard_map/ppermute | solution.py:13
  61.8 6.6 %collective-permute-start.10 = (f32[8,130,1]{1,0,2:T(8,128)S(1)}, f32[8,130,1]{1,0,2:T(8,128)S(1)}, u32[]{:S(2)}, u32[]{:S(2)}) collective-permute-start(f32[8,130,1]{1,0,2:T(8,128)S(1)} %copy.17), channel_id=1, source_target_pairs={{0,4},{4,8},{8,12},{12,16},{16,20},{20,24},{24,28},{1,5},{5,9},{9,... | collective-permute-start | bytes 12488 | tf_op jit(solution)/shard_map/ppermute | solution.py:13
  67.1 6.7 %collective-permute-start.11 = (f32[8,130,1]{1,0,2:T(8,128)S(1)}, f32[8,130,1]{1,0,2:T(8,128)S(1)}, u32[]{:S(2)}, u32[]{:S(2)}) collective-permute-start(f32[8,130,1]{1,0,2:T(8,128)S(1)} %copy.19), channel_id=1, source_target_pairs={{4,0},{8,4},{12,8},{16,12},{20,16},{24,20},{28,24},{5,1},{9,5},{13... | collective-permute-start | bytes 12488 | tf_op jit(solution)/shard_map/ppermute | solution.py:16
  76.8 7.7 %copy-start = (f32[8,128,256]{2,0,1:T(8,128)}, f32[8,128,256]{2,0,1:T(8,128)S(1)}, u32[]{:S(2)}) copy-start(f32[8,128,256]{2,0,1:T(8,128)S(1)} %fusion.27) | copy-start | bytes 3145732
  76.8 6.2 %collective-permute-start.13 = (f32[8,1,256]{2,0,1:T(8,128)S(1)}, f32[8,1,256]{2,0,1:T(8,128)S(1)}, u32[]{:S(2)}, u32[]{:S(2)}) collective-permute-start(f32[8,1,256]{2,0,1:T(8,128)S(1)} %get-tuple-element.19), channel_id=1, source_target_pairs={{32,0},{64,32},{96,64},{128,96},{160,128},{192,160},{224,192},{33,... | collective-permute-start | bytes 24584 | tf_op jit(solution)/shard_map/ppermute | solution.py:16
  78.1 6.3 %collective-permute-start.12 = (f32[8,1,256]{2,0,1:T(8,128)S(1)}, f32[8,1,256]{2,0,1:T(8,128)S(1)}, u32[]{:S(2)}, u32[]{:S(2)}) collective-permute-start(f32[8,1,256]{2,0,1:T(8,128)S(1)} %get-tuple-element.20), channel_id=1, source_target_pairs={{0,32},{32,64},{64,96},{96,128},{128,160},{160,192},{192,224},{1,3... | collective-permute-start | bytes 24584 | tf_op jit(solution)/shard_map/ppermute | solution.py:13
  85.5 8.5 %copy-start.2 = (f32[5]{0:T(128)S(1)}, f32[5]{0:T(128)}, u32[]{:S(2)}) copy-start(f32[5]{0:T(128)} %param.9) | copy-start | bytes 64
  87.2 9.3 %collective-permute-start.15 = (f32[8,130,1]{1,0,2:T(8,128)S(1)}, f32[8,130,1]{1,0,2:T(8,128)S(1)}, u32[]{:S(2)}, u32[]{:S(2)}) collective-permute-start(f32[8,130,1]{1,0,2:T(8,128)S(1)} %copy.23), channel_id=1, source_target_pairs={{4,0},{8,4},{12,8},{16,12},{20,16},{24,20},{28,24},{5,1},{9,5},{13... | collective-permute-start | bytes 12488 | tf_op jit(solution)/shard_map/ppermute | solution.py:16
  88.5 6.8 %collective-permute-start.14 = (f32[8,130,1]{1,0,2:T(8,128)S(1)}, f32[8,130,1]{1,0,2:T(8,128)S(1)}, u32[]{:S(2)}, u32[]{:S(2)}) collective-permute-start(f32[8,130,1]{1,0,2:T(8,128)S(1)} %copy.21), channel_id=1, source_target_pairs={{0,4},{4,8},{8,12},{12,16},{16,20},{20,24},{24,28},{1,5},{5,9},{9,... | collective-permute-start | bytes 12488 | tf_op jit(solution)/shard_map/ppermute | solution.py:13
  106.0 7.3 %collective-permute-start.17 = (f32[8,1,256]{2,0,1:T(8,128)S(1)}, f32[8,1,256]{2,0,1:T(8,128)S(1)}, u32[]{:S(2)}, u32[]{:S(2)}) collective-permute-start(f32[8,1,256]{2,0,1:T(8,128)S(1)} %get-tuple-element.17), channel_id=1, source_target_pairs={{32,0},{64,32},{96,64},{128,96},{160,128},{192,160},{224,192},{33,... | collective-permute-start | bytes 24584 | tf_op jit(solution)/shard_map/ppermute | solution.py:16
  107.3 7.4 %collective-permute-start.16 = (f32[8,1,256]{2,0,1:T(8,128)S(1)}, f32[8,1,256]{2,0,1:T(8,128)S(1)}, u32[]{:S(2)}, u32[]{:S(2)}) collective-permute-start(f32[8,1,256]{2,0,1:T(8,128)S(1)} %get-tuple-element.18), channel_id=1, source_target_pairs={{0,32},{32,64},{64,96},{96,128},{128,160},{160,192},{192,224},{1,3... | collective-permute-start | bytes 24584 | tf_op jit(solution)/shard_map/ppermute | solution.py:13
  115.3 6.7 %collective-permute-start.18 = (f32[8,130,1]{1,0,2:T(8,128)S(1)}, f32[8,130,1]{1,0,2:T(8,128)S(1)}, u32[]{:S(2)}, u32[]{:S(2)}) collective-permute-start(f32[8,130,1]{1,0,2:T(8,128)S(1)} %copy.25), channel_id=1, source_target_pairs={{0,4},{4,8},{8,12},{12,16},{16,20},{20,24},{24,28},{1,5},{5,9},{9,... | collective-permute-start | bytes 12488 | tf_op jit(solution)/shard_map/ppermute | solution.py:13
  120.5 6.7 %collective-permute-start.19 = (f32[8,130,1]{1,0,2:T(8,128)S(1)}, f32[8,130,1]{1,0,2:T(8,128)S(1)}, u32[]{:S(2)}, u32[]{:S(2)}) collective-permute-start(f32[8,130,1]{1,0,2:T(8,128)S(1)} %copy.27), channel_id=1, source_target_pairs={{4,0},{8,4},{12,8},{16,12},{20,16},{24,20},{28,24},{5,1},{9,5},{13... | collective-permute-start | bytes 12488 | tf_op jit(solution)/shard_map/ppermute | solution.py:16
Sparse Core Ops, SparseCore 0:
  131.8 71.4 all-gather.1
where the time goes:
time: 538 us; the launch traced here: 537 us
  blocking collectives  310 us (58%)
  waiting for transfers between devices  90.3 us (17%)
  starting transfers between devices  62.9 us (12%)
  other arithmetic  22.4 us (4%)
  local copies, waits for them, and re-layouts  20.9 us (4%)
  matrix products  16.7 us (3%)
  between operations  14.3 us (3%)
    psum x1, blocking collectives, shards(): total = lax.psum(partial_gram, ('lx', 'ly'))  310 us
    all_gather x1, waiting for transfers between devices, shards(): lax.all_gather(paired, 'blk', axis=1, tiled=True)  71.7 us
    ppermute x10, starting transfers between devices, extended(): lax.ppermute(lax.slice_in_dim(block, block.shape[dim] - width, None, axis...  49.7 us
    dot_general x1, matrix products, gram_rows(): lax.dot_general(flat, search_flat, (((1,), (1,)), ((), ())), precision=la...  16.7 us
    ppermute x10, starting transfers between devices, extended(): lax.ppermute(lax.slice_in_dim(block, 0, width, axis=dim), axis, backward)  13.1 us
  transfers between devices with their start and end apart: 21, of which 11 were waited for; matrix products, arithmetic and copies ran while one was open for 1% of the time, Pallas kernels for 0%

commit v1 on v0

--- a/solution.py
+++ b/solution.py
@@ -64,7 +64,7 @@
     image = scaled_step(padded_field, onsite_energy, present)
     paired = jnp.stack([filtered, image])
     partial_gram = gram_rows(lax.all_gather(paired, "blk", axis=1, tiled=True), search_vectors)
-    total = lax.psum(partial_gram, ("lx", "ly"))
+    total = lax.psum(lax.psum(partial_gram, "lx"), axis_name="ly")
     return total * scale_factor
 
 

time: 538 us -> 294 us (0.55)
  blocking collectives: 310 us -> 65.1 us
    psum x1 -> x2, blocking collectives: 310 us -> 65.1 us  [shards(): total = lax.psum(lax.psum(partial_gram, 'lx'), axis_name='ly')]
  transfers between devices with their start and end apart: 21 -> 21, of which waited for: 11 -> 10; matrix products, arithmetic and copies ran while one was open for 1% -> 2% of each run, Pallas kernels for 0% -> 0%
where the time goes in v1:
time: 294 us; the launch traced here: 293 us
  waiting for transfers between devices  90.2 us (31%)
  blocking collectives  65.1 us (22%)
  starting transfers between devices  62.9 us (21%)
  other arithmetic  22.4 us (8%)
  local copies, waits for them, and re-layouts  21 us (7%)
  matrix products  16.7 us (6%)
  between operations  14.4 us (5%)
    all_gather x1, waiting for transfers between devices, shards(): lax.all_gather(paired, 'blk', axis=1, tiled=True)  71.7 us
    psum x2, blocking collectives, shards(): total = lax.psum(lax.psum(partial_gram, 'lx'), axis_name='ly')  65.1 us
    ppermute x10, starting transfers between devices, extended(): lax.ppermute(lax.slice_in_dim(block, block.shape[dim] - width, None, axis...  49.7 us
    dot_general x1, matrix products, gram_rows(): lax.dot_general(flat, search_flat, (((1,), (1,)), ((), ())), precision=la...  16.7 us
    ppermute x10, starting transfers between devices, extended(): lax.ppermute(lax.slice_in_dim(block, 0, width, axis=dim), axis, backward)  13.1 us
    ppermute x10, waiting for transfers between devices, extended(): lax.ppermute(lax.slice_in_dim(block, 0, width, axis=dim), axis, backward)  9.85 us
    ppermute x10, waiting for transfers between devices, extended(): lax.ppermute(lax.slice_in_dim(block, block.shape[dim] - width, None, axis...  8.71 us
    add x1, other arithmetic, shards(): filtered = filtered + filter_coefs[order] * current  8.34 us
  transfers between devices with their start and end apart: 21, of which 10 were waited for; matrix products, arithmetic and copies ran while one was open for 2% of the time, Pallas kernels for 0%

profile of v1, /device:TPU:16, one launch (start us, length us, event | category | flops | bytes accessed | tf_op | source)
XLA Modules:
  0.0 292.8 jit_solution(2122486373261042074)
XLA Ops:
  7.5 1.8 copy_multiply_fusion
  10.6 4.5 %collective-permute-start = (f32[8,1,256]{2,0,1:T(8,128)S(1)}, f32[8,1,256]{2,0,1:T(8,128)S(1)}, u32[]{:S(2)}, u32[]{:S(2)}) collective-permute-start(f32[8,1,256]{2,0,1:T(8,128)S(1)} %get-tuple-element.26), channel_id=1, source_target_pairs={{0,32},{32,64},{64,96},{96,128},{128,160},{160,192},{192,224},{1,3... | collective-permute-start | bytes 24584 | tf_op jit(solution)/shard_map/ppermute | solution.py:13
  15.2 1.3 collective-permute-done
  18.8 4.5 %collective-permute-start.2 = (f32[8,130,1]{1,0,2:T(8,128)S(1)}, f32[8,130,1]{1,0,2:T(8,128)S(1)}, u32[]{:S(2)}, u32[]{:S(2)}) collective-permute-start(f32[8,130,1]{1,0,2:T(8,128)S(1)} %copy.9), channel_id=1, source_target_pairs={{0,4},{4,8},{8,12},{12,16},{16,20},{20,24},{24,28},{1,5},{5,9},{9,... | collective-permute-start | bytes 12488 | tf_op jit(solution)/shard_map/ppermute | solution.py:13
  27.1 1.9 broadcast_multiply_fusion
  30.4 4.8 %collective-permute-start.4 = (f32[8,1,256]{2,0,1:T(8,128)S(1)}, f32[8,1,256]{2,0,1:T(8,128)S(1)}, u32[]{:S(2)}, u32[]{:S(2)}) collective-permute-start(f32[8,1,256]{2,0,1:T(8,128)S(1)} %get-tuple-element.24), channel_id=1, source_target_pairs={{0,32},{32,64},{64,96},{96,128},{128,160},{160,192},{192,224},{1,3... | collective-permute-start | bytes 24584 | tf_op jit(solution)/shard_map/ppermute | solution.py:13
  35.2 1.3 collective-permute-done.4
  37.6 1.4 copy.13
  40.7 4.8 %collective-permute-start.6 = (f32[8,130,1]{1,0,2:T(8,128)S(1)}, f32[8,130,1]{1,0,2:T(8,128)S(1)}, u32[]{:S(2)}, u32[]{:S(2)}) collective-permute-start(f32[8,130,1]{1,0,2:T(8,128)S(1)} %copy.13), channel_id=1, source_target_pairs={{0,4},{4,8},{8,12},{12,16},{16,20},{20,24},{24,28},{1,5},{5,9},{9,... | collective-permute-start | bytes 12488 | tf_op jit(solution)/shard_map/ppermute | solution.py:13
  49.2 2.6 fusion.34
  53.1 4.8 %collective-permute-start.8 = (f32[8,1,256]{2,0,1:T(8,128)S(1)}, f32[8,1,256]{2,0,1:T(8,128)S(1)}, u32[]{:S(2)}, u32[]{:S(2)}) collective-permute-start(f32[8,1,256]{2,0,1:T(8,128)S(1)} %get-tuple-element.22), channel_id=1, source_target_pairs={{0,32},{32,64},{64,96},{96,128},{128,160},{160,192},{192,224},{1,3... | collective-permute-start | bytes 24584 | tf_op jit(solution)/shard_map/ppermute | solution.py:13
  58.0 1.3 collective-permute-done.8
  60.4 1.4 copy.17
  61.8 5.0 %collective-permute-start.10 = (f32[8,130,1]{1,0,2:T(8,128)S(1)}, f32[8,130,1]{1,0,2:T(8,128)S(1)}, u32[]{:S(2)}, u32[]{:S(2)}) collective-permute-start(f32[8,130,1]{1,0,2:T(8,128)S(1)} %copy.17), channel_id=1, source_target_pairs={{0,4},{4,8},{8,12},{12,16},{16,20},{20,24},{24,28},{1,5},{5,9},{9,... | collective-permute-start | bytes 12488 | tf_op jit(solution)/shard_map/ppermute | solution.py:13
  68.8 5.0 %collective-permute-done.11 = f32[8,130,1]{1,0,2:T(8,128)S(1)} collective-permute-done((f32[8,130,1]{1,0,2:T(8,128)S(1)}, f32[8,130,1]{1,0,2:T(8,128)S(1)}, u32[]{:S(2)}, u32[]{:S(2)}) %collective-permute-start.11) | collective-permute-done | bytes 4192 | tf_op jit(solution)/shard_map/ppermute | solution.py:16
  75.0 1.8 fusion.27
  78.2 4.9 %collective-permute-start.12 = (f32[8,1,256]{2,0,1:T(8,128)S(1)}, f32[8,1,256]{2,0,1:T(8,128)S(1)}, u32[]{:S(2)}, u32[]{:S(2)}) collective-permute-start(f32[8,1,256]{2,0,1:T(8,128)S(1)} %get-tuple-element.20), channel_id=1, source_target_pairs={{0,32},{32,64},{64,96},{96,128},{128,160},{160,192},{192,224},{1,3... | collective-permute-start | bytes 24584 | tf_op jit(solution)/shard_map/ppermute | solution.py:13
  83.1 1.3 collective-permute-done.12
  85.5 1.4 copy.21
  88.6 5.4 %collective-permute-start.14 = (f32[8,130,1]{1,0,2:T(8,128)S(1)}, f32[8,130,1]{1,0,2:T(8,128)S(1)}, u32[]{:S(2)}, u32[]{:S(2)}) collective-permute-start(f32[8,130,1]{1,0,2:T(8,128)S(1)} %copy.21), channel_id=1, source_target_pairs={{0,4},{4,8},{8,12},{12,16},{16,20},{20,24},{24,28},{1,5},{5,9},{9,... | collective-permute-start | bytes 12488 | tf_op jit(solution)/shard_map/ppermute | solution.py:13
  97.7 8.3 %fusion.20 = f32[8,128,256]{2,0,1:T(8,128)S(1)} fusion(f32[8,128,256]{2,0,1:T(8,128)S(1)} %fusion.34, f32[8,128,256]{2,0,1:T(8,128)} %copy-done, f32[8,1,256]{2,0,1:T(8,128)S(1)} %collective-permute-done.12, f32[8,1,256]{2,0,1:T(8,128)S(1)} %collective-permute-done.13, f32[8,130,1]{2,0,1:T(8,128)} %copy.24, f32[8,130,1]{2,0,1:T(8,128)} %copy.22, ...), kind=kLoop, calls=%fused_computation.33 | loop fusion | flops 6815744 | bytes 5562516 | tf_op jit(solution)/shard_map/add | solution.py:60
  107.4 6.0 %collective-permute-start.16 = (f32[8,1,256]{2,0,1:T(8,128)S(1)}, f32[8,1,256]{2,0,1:T(8,128)S(1)}, u32[]{:S(2)}, u32[]{:S(2)}) collective-permute-start(f32[8,1,256]{2,0,1:T(8,128)S(1)} %get-tuple-element.18), channel_id=1, source_target_pairs={{0,32},{32,64},{64,96},{96,128},{128,160},{160,192},{192,224},{1,3... | collective-permute-start | bytes 24584 | tf_op jit(solution)/shard_map/ppermute | solution.py:13
  113.5 1.3 collective-permute-done.16
  115.4 4.8 %collective-permute-start.18 = (f32[8,130,1]{1,0,2:T(8,128)S(1)}, f32[8,130,1]{1,0,2:T(8,128)S(1)}, u32[]{:S(2)}, u32[]{:S(2)}) collective-permute-start(f32[8,130,1]{1,0,2:T(8,128)S(1)} %copy.25), channel_id=1, source_target_pairs={{0,4},{4,8},{8,12},{12,16},{16,20},{20,24},{24,28},{1,5},{5,9},{9,... | collective-permute-start | bytes 12488 | tf_op jit(solution)/shard_map/ppermute | solution.py:13
  120.6 1.5 collective-permute-start.19
  122.5 4.8 %collective-permute-done.19 = f32[8,130,1]{1,0,2:T(8,128)S(1)} collective-permute-done((f32[8,130,1]{1,0,2:T(8,128)S(1)}, f32[8,130,1]{1,0,2:T(8,128)S(1)}, u32[]{:S(2)}, u32[]{:S(2)}) %collective-permute-start.19) | collective-permute-done | bytes 4192 | tf_op jit(solution)/shard_map/ppermute | solution.py:16
  128.5 1.8 fusion.11
  130.3 1.5 pad_maximum_fusion
  131.8 71.7 %all-gather.2.cloned.1.call-done = f32[2,32,128,256]{3,1,2,0:T(8,128)} async-done(((f32[2,8,128,256]{3,1,2,0:T(8,128)}), f32[2,32,128,256]{3,1,2,0:T(8,128)}) %all-gather.2.cloned.1.call-update) | async-done | bytes 8388624 | tf_op jit(solution)/shard_map/all_gather | solution.py:66
  203.5 16.7 %fusion.3 = f32[2,32,64]{2,1,0:T(8,128)S(1)} fusion(f32[2,32,128,256]{3,1,2,0:T(8,128)} %all-gather.2.cloned.1.call-done, f32[64,128,256]{2,1,0:T(8,128)} %param.6), kind=kOutput, calls=%fused_computation.4 | convolution fusion | flops 1610612736 | bytes 16793600 | tf_op jit(solution)/shard_map/dot_general | solution.py:39
  220.2 30.4 %psum.14 = f32[2,32,64]{2,1,0:T(8,128)S(1)} all-reduce(f32[2,32,64]{2,1,0:T(8,128)S(1)} %fusion.3), channel_id=1, replica_groups=mesh['lx'=8,'ly'=8,'blk'=4] {'lx'}, use_global_device_ids=true, to_apply=%region_0.1 | all-reduce | flops 4096 | bytes 32768 | tf_op jit(solution)/shard_map/psum | solution.py:67
  250.6 34.7 %psum.15 = f32[2,32,64]{2,1,0:T(8,128)S(1)} all-reduce(f32[2,32,64]{2,1,0:T(8,128)S(1)} %psum.14), channel_id=1, replica_groups=mesh['lx'=8,'ly'=8,'blk'=4] {'ly'}, use_global_device_ids=true, to_apply=%region_1.2 | all-reduce | flops 4096 | bytes 32768 | tf_op jit(solution)/shard_map/psum | solution.py:67
  (67 shorter events, 33.1 us)
Async XLA Ops:
  6.5 197.0 %all-gather.2.cloned.1.call-start = ((), (), s32[]{:S(2)}) async-start(), calls=%async_computation | async-start | bytes 10485760 | tf_op jit(solution)/shard_map/all_gather | solution.py:66
  9.3 5.9 %collective-permute-start.1 = (f32[8,1,256]{2,0,1:T(8,128)S(1)}, f32[8,1,256]{2,0,1:T(8,128)S(1)}, u32[]{:S(2)}, u32[]{:S(2)}) collective-permute-start(f32[8,1,256]{2,0,1:T(8,128)S(1)} %get-tuple-element.25), channel_id=1, source_target_pairs={{32,0},{64,32},{96,64},{128,96},{160,128},{192,160},{224,192},{33,... | collective-permute-start | bytes 24584 | tf_op jit(solution)/shard_map/ppermute | solution.py:16
  10.6 5.9 %collective-permute-start = (f32[8,1,256]{2,0,1:T(8,128)S(1)}, f32[8,1,256]{2,0,1:T(8,128)S(1)}, u32[]{:S(2)}, u32[]{:S(2)}) collective-permute-start(f32[8,1,256]{2,0,1:T(8,128)S(1)} %get-tuple-element.26), channel_id=1, source_target_pairs={{0,32},{32,64},{64,96},{96,128},{128,160},{160,192},{192,224},{1,3... | collective-permute-start | bytes 24584 | tf_op jit(solution)/shard_map/ppermute | solution.py:13
  16.8 10.3 %copy-start.1 = (f32[128,256]{1,0:T(8,128)S(1)}, f32[128,256]{1,0:T(8,128)}, u32[]{:S(2)}) copy-start(f32[128,256]{1,0:T(8,128)} %param.7) | copy-start | bytes 393220
  17.5 8.4 %collective-permute-start.3 = (f32[8,130,1]{1,0,2:T(8,128)S(1)}, f32[8,130,1]{1,0,2:T(8,128)S(1)}, u32[]{:S(2)}, u32[]{:S(2)}) collective-permute-start(f32[8,130,1]{1,0,2:T(8,128)S(1)} %copy.11), channel_id=1, source_target_pairs={{4,0},{8,4},{12,8},{16,12},{20,16},{24,20},{28,24},{5,1},{9,5},{13... | collective-permute-start | bytes 12488 | tf_op jit(solution)/shard_map/ppermute | solution.py:16
  18.8 5.9 %collective-permute-start.2 = (f32[8,130,1]{1,0,2:T(8,128)S(1)}, f32[8,130,1]{1,0,2:T(8,128)S(1)}, u32[]{:S(2)}, u32[]{:S(2)}) collective-permute-start(f32[8,130,1]{1,0,2:T(8,128)S(1)} %copy.9), channel_id=1, source_target_pairs={{0,4},{4,8},{8,12},{12,16},{16,20},{20,24},{24,28},{1,5},{5,9},{9,... | collective-permute-start | bytes 12488 | tf_op jit(solution)/shard_map/ppermute | solution.py:13
  29.1 6.1 %collective-permute-start.5 = (f32[8,1,256]{2,0,1:T(8,128)S(1)}, f32[8,1,256]{2,0,1:T(8,128)S(1)}, u32[]{:S(2)}, u32[]{:S(2)}) collective-permute-start(f32[8,1,256]{2,0,1:T(8,128)S(1)} %get-tuple-element.23), channel_id=1, source_target_pairs={{32,0},{64,32},{96,64},{128,96},{160,128},{192,160},{224,192},{33,... | collective-permute-start | bytes 24584 | tf_op jit(solution)/shard_map/ppermute | solution.py:16
  30.4 6.2 %collective-permute-start.4 = (f32[8,1,256]{2,0,1:T(8,128)S(1)}, f32[8,1,256]{2,0,1:T(8,128)S(1)}, u32[]{:S(2)}, u32[]{:S(2)}) collective-permute-start(f32[8,1,256]{2,0,1:T(8,128)S(1)} %get-tuple-element.24), channel_id=1, source_target_pairs={{0,32},{32,64},{64,96},{96,128},{128,160},{160,192},{192,224},{1,3... | collective-permute-start | bytes 24584 | tf_op jit(solution)/shard_map/ppermute | solution.py:13
  39.4 8.7 %collective-permute-start.7 = (f32[8,130,1]{1,0,2:T(8,128)S(1)}, f32[8,130,1]{1,0,2:T(8,128)S(1)}, u32[]{:S(2)}, u32[]{:S(2)}) collective-permute-start(f32[8,130,1]{1,0,2:T(8,128)S(1)} %copy.15), channel_id=1, source_target_pairs={{4,0},{8,4},{12,8},{16,12},{20,16},{24,20},{28,24},{5,1},{9,5},{13... | collective-permute-start | bytes 12488 | tf_op jit(solution)/shard_map/ppermute | solution.py:16
  40.7 6.2 %collective-permute-start.6 = (f32[8,130,1]{1,0,2:T(8,128)S(1)}, f32[8,130,1]{1,0,2:T(8,128)S(1)}, u32[]{:S(2)}, u32[]{:S(2)}) collective-permute-start(f32[8,130,1]{1,0,2:T(8,128)S(1)} %copy.13), channel_id=1, source_target_pairs={{0,4},{4,8},{8,12},{12,16},{16,20},{20,24},{24,28},{1,5},{5,9},{9,... | collective-permute-start | bytes 12488 | tf_op jit(solution)/shard_map/ppermute | solution.py:13
  51.8 6.1 %collective-permute-start.9 = (f32[8,1,256]{2,0,1:T(8,128)S(1)}, f32[8,1,256]{2,0,1:T(8,128)S(1)}, u32[]{:S(2)}, u32[]{:S(2)}) collective-permute-start(f32[8,1,256]{2,0,1:T(8,128)S(1)} %get-tuple-element.21), channel_id=1, source_target_pairs={{32,0},{64,32},{96,64},{128,96},{160,128},{192,160},{224,192},{33,... | collective-permute-start | bytes 24584 | tf_op jit(solution)/shard_map/ppermute | solution.py:16
  53.1 6.2 %collective-permute-start.8 = (f32[8,1,256]{2,0,1:T(8,128)S(1)}, f32[8,1,256]{2,0,1:T(8,128)S(1)}, u32[]{:S(2)}, u32[]{:S(2)}) collective-permute-start(f32[8,1,256]{2,0,1:T(8,128)S(1)} %get-tuple-element.22), channel_id=1, source_target_pairs={{0,32},{32,64},{64,96},{96,128},{128,160},{160,192},{192,224},{1,3... | collective-permute-start | bytes 24584 | tf_op jit(solution)/shard_map/ppermute | solution.py:13
  61.8 6.6 %collective-permute-start.10 = (f32[8,130,1]{1,0,2:T(8,128)S(1)}, f32[8,130,1]{1,0,2:T(8,128)S(1)}, u32[]{:S(2)}, u32[]{:S(2)}) collective-permute-start(f32[8,130,1]{1,0,2:T(8,128)S(1)} %copy.17), channel_id=1, source_target_pairs={{0,4},{4,8},{8,12},{12,16},{16,20},{20,24},{24,28},{1,5},{5,9},{9,... | collective-permute-start | bytes 12488 | tf_op jit(solution)/shard_map/ppermute | solution.py:13
  67.1 6.7 %collective-permute-start.11 = (f32[8,130,1]{1,0,2:T(8,128)S(1)}, f32[8,130,1]{1,0,2:T(8,128)S(1)}, u32[]{:S(2)}, u32[]{:S(2)}) collective-permute-start(f32[8,130,1]{1,0,2:T(8,128)S(1)} %copy.19), channel_id=1, source_target_pairs={{4,0},{8,4},{12,8},{16,12},{20,16},{24,20},{28,24},{5,1},{9,5},{13... | collective-permute-start | bytes 12488 | tf_op jit(solution)/shard_map/ppermute | solution.py:16
  76.8 7.7 %copy-start = (f32[8,128,256]{2,0,1:T(8,128)}, f32[8,128,256]{2,0,1:T(8,128)S(1)}, u32[]{:S(2)}) copy-start(f32[8,128,256]{2,0,1:T(8,128)S(1)} %fusion.27) | copy-start | bytes 3145732
  76.8 6.2 %collective-permute-start.13 = (f32[8,1,256]{2,0,1:T(8,128)S(1)}, f32[8,1,256]{2,0,1:T(8,128)S(1)}, u32[]{:S(2)}, u32[]{:S(2)}) collective-permute-start(f32[8,1,256]{2,0,1:T(8,128)S(1)} %get-tuple-element.19), channel_id=1, source_target_pairs={{32,0},{64,32},{96,64},{128,96},{160,128},{192,160},{224,192},{33,... | collective-permute-start | bytes 24584 | tf_op jit(solution)/shard_map/ppermute | solution.py:16
  78.2 6.3 %collective-permute-start.12 = (f32[8,1,256]{2,0,1:T(8,128)S(1)}, f32[8,1,256]{2,0,1:T(8,128)S(1)}, u32[]{:S(2)}, u32[]{:S(2)}) collective-permute-start(f32[8,1,256]{2,0,1:T(8,128)S(1)} %get-tuple-element.20), channel_id=1, source_target_pairs={{0,32},{32,64},{64,96},{96,128},{128,160},{160,192},{192,224},{1,3... | collective-permute-start | bytes 24584 | tf_op jit(solution)/shard_map/ppermute | solution.py:13
  85.5 8.5 %copy-start.2 = (f32[5]{0:T(128)S(1)}, f32[5]{0:T(128)}, u32[]{:S(2)}) copy-start(f32[5]{0:T(128)} %param.9) | copy-start | bytes 64
  87.3 9.3 %collective-permute-start.15 = (f32[8,130,1]{1,0,2:T(8,128)S(1)}, f32[8,130,1]{1,0,2:T(8,128)S(1)}, u32[]{:S(2)}, u32[]{:S(2)}) collective-permute-start(f32[8,130,1]{1,0,2:T(8,128)S(1)} %copy.23), channel_id=1, source_target_pairs={{4,0},{8,4},{12,8},{16,12},{20,16},{24,20},{28,24},{5,1},{9,5},{13... | collective-permute-start | bytes 12488 | tf_op jit(solution)/shard_map/ppermute | solution.py:16
  88.6 6.8 %collective-permute-start.14 = (f32[8,130,1]{1,0,2:T(8,128)S(1)}, f32[8,130,1]{1,0,2:T(8,128)S(1)}, u32[]{:S(2)}, u32[]{:S(2)}) collective-permute-start(f32[8,130,1]{1,0,2:T(8,128)S(1)} %copy.21), channel_id=1, source_target_pairs={{0,4},{4,8},{8,12},{12,16},{16,20},{20,24},{24,28},{1,5},{5,9},{9,... | collective-permute-start | bytes 12488 | tf_op jit(solution)/shard_map/ppermute | solution.py:13
  106.1 7.3 %collective-permute-start.17 = (f32[8,1,256]{2,0,1:T(8,128)S(1)}, f32[8,1,256]{2,0,1:T(8,128)S(1)}, u32[]{:S(2)}, u32[]{:S(2)}) collective-permute-start(f32[8,1,256]{2,0,1:T(8,128)S(1)} %get-tuple-element.17), channel_id=1, source_target_pairs={{32,0},{64,32},{96,64},{128,96},{160,128},{192,160},{224,192},{33,... | collective-permute-start | bytes 24584 | tf_op jit(solution)/shard_map/ppermute | solution.py:16
  107.4 7.4 %collective-permute-start.16 = (f32[8,1,256]{2,0,1:T(8,128)S(1)}, f32[8,1,256]{2,0,1:T(8,128)S(1)}, u32[]{:S(2)}, u32[]{:S(2)}) collective-permute-start(f32[8,1,256]{2,0,1:T(8,128)S(1)} %get-tuple-element.18), channel_id=1, source_target_pairs={{0,32},{32,64},{64,96},{96,128},{128,160},{160,192},{192,224},{1,3... | collective-permute-start | bytes 24584 | tf_op jit(solution)/shard_map/ppermute | solution.py:13
  115.4 6.7 %collective-permute-start.18 = (f32[8,130,1]{1,0,2:T(8,128)S(1)}, f32[8,130,1]{1,0,2:T(8,128)S(1)}, u32[]{:S(2)}, u32[]{:S(2)}) collective-permute-start(f32[8,130,1]{1,0,2:T(8,128)S(1)} %copy.25), channel_id=1, source_target_pairs={{0,4},{4,8},{8,12},{12,16},{16,20},{20,24},{24,28},{1,5},{5,9},{9,... | collective-permute-start | bytes 12488 | tf_op jit(solution)/shard_map/ppermute | solution.py:13
  120.6 6.7 %collective-permute-start.19 = (f32[8,130,1]{1,0,2:T(8,128)S(1)}, f32[8,130,1]{1,0,2:T(8,128)S(1)}, u32[]{:S(2)}, u32[]{:S(2)}) collective-permute-start(f32[8,130,1]{1,0,2:T(8,128)S(1)} %copy.27), channel_id=1, source_target_pairs={{4,0},{8,4},{12,8},{16,12},{20,16},{24,20},{28,24},{5,1},{9,5},{13... | collective-permute-start | bytes 12488 | tf_op jit(solution)/shard_map/ppermute | solution.py:16
Sparse Core Ops, SparseCore 0:
  131.9 71.4 all-gather.1
